TPU v7x, 256 devices: a whole 4x4x8 slice. The times are simulated.
256 devices in a mesh: dp: 4 (over x), expert: 64 (over y, z, core).
Axes of the slice: x: 4, y: 4, z: 8, core: 2. Of those that a mesh axis runs over, the one named last changes fastest.
Arguments:
- tokens: bfloat16 [8192, 4096], P('expert', 'dp'), may hold values from -6 to 6
- routes: int32 [8192, 4], P('expert'), may hold values from 0 to 63, all different within a row; in each aligned block of 128 rows (0 to 127, 128 to 255, ...) at most 16 rows name the same one
- route_weights: float32 [8192, 4], P('expert'), may hold values from 0.1 to 1
- gate_weight: bfloat16 [64, 4096, 1536], P('expert', None, 'dp'), may hold values from -0.09375 to 0.09375
- up_weight: bfloat16 [64, 4096, 1536], P('expert', None, 'dp'), may hold values from -0.09375 to 0.09375
- down_weight: bfloat16 [64, 1536, 4096], P('expert', 'dp'), may hold values from -0.15625 to 0.15625
- sketch_basis: bfloat16 [1536, 128], P('dp'), may hold values from -0.15625 to 0.15625
Outputs:
- mixed: bfloat16 [8192, 4096], P('expert', 'dp')
- sketch: float32 [64, 128, 1536], P('expert', None, 'dp')
Inputs may be any that keep to these rules, and one draw needn't show every extreme that they name: `routes`: each row names 4 different experts; within the rows of one device no expert is named more than 16 times, a bound that some block reaches.
All inputs are finite; a program needn't handle non-finite values.
Results may differ from a plain program's by a relative error of at most 0.017.
Values may be sent and summed in bfloat16 or wider, within the bound.
No kernel may reach another device: no remote copies, remote signals or barrier semaphores. Data moves between devices by JAX's collectives and lax.ppermute only.
A program may use at most 128 MiB of HBM per device.

v0:
```python
import jax
import jax.numpy as jnp
from jax import lax
from jax.sharding import PartitionSpec as P

ridge_term = 1.0


def gram_matrix(factor_rows):
    return jnp.dot(factor_rows.T, factor_rows, precision=lax.Precision.HIGHEST)


def body(tokens, routes, route_weights, gate_weight, up_weight, down_weight, sketch_basis):
    owners = lax.axis_size("expert")
    token_count, route_count = routes.shape
    pair_count = token_count * route_count
    capacity = 2 * pair_count // owners
    slot_total = owners * capacity
    route_list = routes.reshape(-1)
    onehot = (route_list[:, None] == jnp.arange(owners, dtype=jnp.int32)[None, :]).astype(jnp.int32)
    before = jnp.cumsum(onehot, axis=0) - onehot
    slot_of = jnp.sum(before * onehot, axis=1)
    counts = jnp.sum(onehot, axis=0)
    target = route_list * capacity + slot_of
    source_pair = (
        jnp.zeros((slot_total,), jnp.int32).at[target].set(jnp.arange(pair_count, dtype=jnp.int32))
    )
    source_token = source_pair // route_count
    count_wire = counts.astype(jnp.bfloat16)
    features = lax.all_gather(tokens, "dp", axis=1, tiled=True)
    outgoing = features[source_token].reshape(owners, capacity, features.shape[1])
    arrived, arrived_counts = (
        lax.all_to_all(outgoing, "expert", split_axis=0, concat_axis=0, tiled=True),
        lax.all_to_all(count_wire, "expert", split_axis=0, concat_axis=0, tiled=True),
    )
    width = arrived.shape[2]
    live_count = arrived_counts.astype(jnp.int32)
    live_mask = (jnp.arange(capacity, dtype=jnp.int32)[None, :] < live_count[:, None]).reshape(-1)
    slot_rows = jnp.where(
        live_mask[:, None], arrived.reshape(slot_total, width), jnp.zeros((), jnp.bfloat16)
    )
    gate_local = gate_weight[0]
    up_local = up_weight[0]
    down_local = down_weight[0]
    gate_val = jnp.dot(slot_rows, gate_local, preferred_element_type=jnp.float32)
    up_val = jnp.dot(slot_rows, up_local, preferred_element_type=jnp.float32)
    hidden_block = (jax.nn.silu(gate_val) * up_val).astype(jnp.bfloat16)
    partial_value = jnp.dot(hidden_block, down_local, preferred_element_type=jnp.float32)
    sums = lax.psum_scatter(
        partial_value.reshape(owners, capacity, width).astype(jnp.bfloat16),
        "dp",
        scatter_dimension=2,
        tiled=True,
    )
    returned = lax.all_to_all(sums, "expert", split_axis=0, concat_axis=0, tiled=True)
    picked = returned.reshape(slot_total, returned.shape[2])[target]
    weighted = jnp.einsum(
        "tkd,tk->td",
        picked.reshape(token_count, route_count, returned.shape[2]).astype(jnp.float32),
        route_weights,
    )
    mixed = weighted.astype(jnp.bfloat16)
    sketch_part = jnp.dot(hidden_block, sketch_basis, preferred_element_type=jnp.float32)
    sketch_width = sketch_part.shape[1]
    eye_matrix = jnp.eye(sketch_width, dtype=jnp.float32)
    sketch_full = lax.psum(sketch_part.astype(jnp.bfloat16), "dp").astype(jnp.float32)
    lower_factor = jnp.linalg.cholesky(gram_matrix(sketch_full) + ridge_term * eye_matrix)
    projected = jnp.dot(
        sketch_full.T, hidden_block.astype(jnp.float32), precision=lax.Precision.HIGHEST
    )
    whitened = jax.scipy.linalg.solve_triangular(lower_factor, projected, lower=True)
    return (mixed, whitened[None])


def solution(mesh):
    return jax.shard_map(
        body,
        mesh=mesh,
        in_specs=(
            P("expert", "dp"),
            P("expert", None),
            P("expert", None),
            P("expert", None, "dp"),
            P("expert", None, "dp"),
            P("expert", "dp", None),
            P("dp", None),
        ),
        out_specs=(P("expert", "dp"), P("expert", None, "dp")),
        check_vma=False,
    )
```

profile of v0, /device:TPU:8, one launch (start us, length us, event | category | flops | bytes accessed | tf_op | source)
XLA Modules:
  0.0 463.0 jit_solution(337429624355263726)
XLA Ops:
  7.2 0.0 copy-start
  7.2 0.0 all-gather.2.cloned.1.call-start
  7.2 0.7 all-gather.2.cloned.1.call-update
  7.9 1.0 copy.21
  8.9 0.1 eq.33
  9.0 0.1 eq.29
  9.1 1.2 reduce-window.6
  10.3 0.2 slice_reduce_fusion
  10.6 0.2 convert_reduce_fusion
  10.8 0.7 copy.22
  11.5 12.1 %all-to-all-start = ((bf16[64,1,1]{2,1,0:T(2,128)(2,1)}), bf16[64,1,1]{2,1,0:T(2,128)(2,1)S(1)}, u32[]{:S(2)}, u32[]{:S(2)}) async-start(bf16[64,1,1]{2,1,0:T(2,128)(2,1)} %copy.22), calls=%async_computation | async-start | bytes 65536 | tf_op jit(solution)/shard_map/all_to_all | solution.py:34
  23.6 0.7 broadcast_multiply_fusion
  24.3 0.1 copy.23
  24.5 0.1 mul.28
  24.6 2.4 scatter_custom_fusion
  27.1 12.2 %all-gather.2.cloned.1.call-done = bf16[128,4096]{1,0:T(8,128)(2,1)} async-done(((bf16[128,1024]{1,0:T(8,128)(2,1)}), bf16[128,4096]{1,0:T(8,128)(2,1)}) %all-gather.2.cloned.1.call-update) | async-done | bytes 1048592 | tf_op jit(solution)/shard_map/all_gather | solution.py:30
  39.2 16.4 %gather_fusion = bf16[1024,4096]{1,0:T(8,128)(2,1)} fusion(bf16[128,4096]{1,0:T(8,128)(2,1)} %all-gather.2.cloned.1.call-done, s32[1024]{0:T(1024)S(1)} %fusion.15), kind=kCustom, calls=%fused_computation | custom fusion | bytes 16781312 | tf_op jit(solution)/shard_map/gather | solution.py:31
  55.7 10.8 %all-to-all-start.1 = ((bf16[64,16,4096]{2,1,0:T(8,128)(2,1)}), bf16[64,16,4096]{2,1,0:T(8,128)(2,1)}, u32[]{:S(2)}, u32[]{:S(2)}) async-start(bf16[64,16,4096]{2,1,0:T(8,128)(2,1)} %bitcast.60), calls=%async_computation.1 | async-start | bytes 16777216 | tf_op jit(solution)/shard_map/all_to_all | solution.py:33
  66.4 0.2 reduce-scatter.2.cloned.1.call-start
  66.7 1.2 convert_reduce_fusion.1
  67.9 0.1 iota_compare_fusion.5
  68.0 182.8 %all-to-all-done.1 = bf16[64,16,4096]{2,1,0:T(8,128)(2,1)} async-done(((bf16[64,16,4096]{2,1,0:T(8,128)(2,1)}), bf16[64,16,4096]{2,1,0:T(8,128)(2,1)}, u32[]{:S(2)}, u32[]{:S(2)}) %all-to-all-start.1) | async-done | bytes 8388640 | tf_op jit(solution)/shard_map/all_to_all | solution.py:33
  250.8 7.2 %broadcast_select_fusion = bf16[64,16,4096]{2,1,0:T(8,128)(2,1)} fusion(bf16[64,16,4096]{2,1,0:T(8,128)(2,1)} %all-to-all-done.1, pred[64,16]{1,0:T(8,128)(4,1)S(1)} %iota_compare_fusion.5), kind=kLoop, calls=%fused_computation.3 | loop fusion | flops 4194304 | bytes 16778240 | tf_op jit(solution)/shard_map/jit(_where)/select_n | solution.py:39
  258.0 8.0 %fusion.3 = f32[1024,384]{1,0:T(8,128)S(1)} fusion(bf16[1024,4096]{1,0:T(8,128)(2,1)} %bitcast.61, bf16[1,4096,384]{2,1,0:T(8,128)(2,1)} %param.10), kind=kOutput, calls=%fused_computation.8 | convolution fusion | flops 3221225472 | bytes 13107200 | tf_op jit(solution)/shard_map/dot_general | solution.py:45
  266.0 4.6 multiply_convert_fusion
  270.6 0.9 copy-done.2
  271.5 6.6 %convolution_convert_fusion = bf16[64,16,4096]{2,1,0:T(8,128)(2,1)} fusion(bf16[64,16,384]{2,1,0:T(8,128)(2,1)S(1)} %bitcast.63, bf16[1,384,4096]{2,1,0:T(8,128)(2,1)S(1)} %copy-done), kind=kOutput, calls=%fused_computation.4 | convolution fusion | flops 3225419776 | bytes 12320768 | tf_op jit(solution)/shard_map/dot_general | solution.py:48
  278.1 0.0 reduce-scatter.2.cloned.1.call-update
  278.1 0.0 copy-start.3
  278.2 80.3 %reduce-scatter.2.cloned.1.call-done = bf16[64,16,1024]{2,1,0:T(8,128)(2,1)} async-done(((bf16[64,16,4096]{2,1,0:T(8,128)(2,1)}), bf16[64,16,1024]{2,1,0:T(8,128)(2,1)}) %reduce-scatter.2.cloned.1.call-update) | async-done | bytes 2097168 | tf_op jit(solution)/shard_map/reduce_scatter | solution.py:49
  358.5 10.8 %all-to-all-start.2 = ((bf16[64,16,1024]{2,1,0:T(8,128)(2,1)}), bf16[64,16,1024]{2,1,0:T(8,128)(2,1)}, u32[]{:S(2)}, u32[]{:S(2)}) async-start(bf16[64,16,1024]{2,1,0:T(8,128)(2,1)} %reduce-scatter.2.cloned.1.call-done), calls=%async_computation.3 | async-start | bytes 4194304 | tf_op jit(solution)/shard_map/all_to_all | solution.py:55
  369.2 0.3 all-reduce.2.cloned.1.call-start
  369.5 2.2 convolution_convert_fusion.1
  371.7 0.0 all-reduce.2.cloned.1.call-update
  371.7 0.2 copy.27
  371.9 47.3 %all-reduce.2.cloned.1.call-done = bf16[1024,128]{1,0:T(8,128)(2,1)} async-done(((bf16[1024,128]{1,0:T(8,128)(2,1)}), bf16[1024,128]{1,0:T(8,128)(2,1)}) %all-reduce.2.cloned.1.call-update) | async-done | bytes 262160 | tf_op jit(solution)/shard_map/psum | solution.py:66
  419.2 1.3 fusion.20
  420.5 0.1 copy.26
  420.7 11.7 %cholesky.17 = f32[128,128]{1,0:T(8,128)S(1)} custom-call(f32[128,128]{1,0:T(8,128)S(1)} %fusion.13), custom_call_target="Cholesky" | custom-call | tf_op jit(solution)/shard_map/jit(cholesky)/cholesky | solution.py:67
  432.4 0.6 compare_reduce_fusion
  433.1 0.7 fusion.10
  433.7 9.8 %custom-call.7 = f32[1,128,128]{1,2,0:T(8,128)S(1)} custom-call(f32[1,128,128]{2,1,0:T(8,128)S(1)} %fusion.10), custom_call_target="InvertDiagBlocksLowerTriangular" | custom-call | tf_op jit(solution)/shard_map/jit(_solve_triangular)/triangular_solve | solution.py:71
  443.5 1.5 fusion.21
  445.1 1.0 convolution_bitcast_fusion
  446.1 5.3 %gather_fusion.1 = bf16[512,1024]{1,0:T(8,128)(2,1)} fusion(bf16[1024,1024]{1,0:T(8,128)(2,1)} %bitcast.11, s32[1024]{0:T(1024)S(1)} %pad_clamp_fusion), kind=kCustom, calls=%fused_computation.1 | custom fusion | bytes 2099200 | tf_op jit(solution)/shard_map/gather | solution.py:56
  451.5 2.3 reshape.115
  453.7 1.9 fusion.19
  455.7 0.8 copy.32
  (21 shorter events, 0.2 us)
Async XLA Ops:
  7.2 264.3 %copy-start = (bf16[1,384,4096]{2,1,0:T(8,128)(2,1)S(1)}, bf16[1,384,4096]{2,1,0:T(8,128)(2,1)}, u32[]{:S(2)}) copy-start(bf16[1,384,4096]{2,1,0:T(8,128)(2,1)} %param.12) | copy-start | bytes 9437188
  7.2 32.0 %all-gather.2.cloned.1.call-start = ((), (), s32[]{:S(2)}) async-start(), calls=%async_computation.4 | async-start | bytes 1310720 | tf_op jit(solution)/shard_map/all_gather | solution.py:30
  11.5 44.1 %all-to-all-start = ((bf16[64,1,1]{2,1,0:T(2,128)(2,1)}), bf16[64,1,1]{2,1,0:T(2,128)(2,1)S(1)}, u32[]{:S(2)}, u32[]{:S(2)}) async-start(bf16[64,1,1]{2,1,0:T(2,128)(2,1)} %copy.22), calls=%async_computation | async-start | bytes 65536 | tf_op jit(solution)/shard_map/all_to_all | solution.py:34
  55.7 195.1 %all-to-all-start.1 = ((bf16[64,16,4096]{2,1,0:T(8,128)(2,1)}), bf16[64,16,4096]{2,1,0:T(8,128)(2,1)}, u32[]{:S(2)}, u32[]{:S(2)}) async-start(bf16[64,16,4096]{2,1,0:T(8,128)(2,1)} %bitcast.60), calls=%async_computation.1 | async-start | bytes 16777216 | tf_op jit(solution)/shard_map/all_to_all | solution.py:33
  66.4 292.0 %reduce-scatter.2.cloned.1.call-start = ((), (), s32[]{:S(2)}) async-start(), calls=%async_computation.5 | async-start | bytes 10485760 | tf_op jit(solution)/shard_map/reduce_scatter | solution.py:49
  258.0 8.0 %copy-start.1 = (bf16[64,16,4096]{2,1,0:T(8,128)(2,1)S(1)}, bf16[64,16,4096]{2,1,0:T(8,128)(2,1)}, u32[]{:S(2)}) copy-start(bf16[64,16,4096]{2,1,0:T(8,128)(2,1)} %broadcast_select_fusion) | copy-start | bytes 25165828
  258.0 8.0 %copy-start.5 = (bf16[1,4096,384]{2,1,0:T(8,128)(2,1)S(1)}, bf16[1,4096,384]{2,1,0:T(8,128)(2,1)}, u32[]{:S(2)}) copy-start(bf16[1,4096,384]{2,1,0:T(8,128)(2,1)} %param.11) | copy-start | bytes 9437188
  270.6 0.9 copy-start.2
  278.1 91.4 %copy-start.3 = (bf16[384,128]{1,0:T(8,128)(2,1)S(1)}, bf16[384,128]{1,0:T(8,128)(2,1)}, u32[]{:S(2)}) copy-start(bf16[384,128]{1,0:T(8,128)(2,1)} %param.13) | copy-start | bytes 294916
  278.2 93.6 %copy-start.4 = (f32[128,4]{0,1:T(4,128)S(1)}, f32[128,4]{0,1:T(4,128)}, u32[]{:S(2)}) copy-start(f32[128,4]{0,1:T(4,128)} %param.9) | copy-start | bytes 6148
  358.5 87.7 %all-to-all-start.2 = ((bf16[64,16,1024]{2,1,0:T(8,128)(2,1)}), bf16[64,16,1024]{2,1,0:T(8,128)(2,1)}, u32[]{:S(2)}, u32[]{:S(2)}) async-start(bf16[64,16,1024]{2,1,0:T(8,128)(2,1)} %reduce-scatter.2.cloned.1.call-done), calls=%async_computation.3 | async-start | bytes 4194304 | tf_op jit(solution)/shard_map/all_to_all | solution.py:55
  369.2 50.0 %all-reduce.2.cloned.1.call-start = ((), (), s32[]{:S(2)}) async-start(), calls=%async_computation.6 | async-start | bytes 524288 | tf_op jit(solution)/shard_map/psum | solution.py:66
Sparse Core Ops, SparseCore 0:
  9.8 29.3 all-gather.1
  278.3 80.1 reduce-scatter.1
  373.0 46.2 all-reduce.1
where the time goes:
time: 464 us; the launch traced here: 463 us
  waiting for transfers between devices  323 us (70%)
  starting transfers between devices  34.1 us (7%)
  other arithmetic  33.6 us (7%)
  local copies, waits for them, and re-layouts  30.8 us (7%)
  matrix products  27.2 us (6%)
  between operations  14 us (3%)
    all_to_all x1, waiting for transfers between devices, body(): lax.all_to_all(outgoing, 'expert', split_axis=0, concat_axis=0, tiled=True)  183 us
    reduce_scatter x1, waiting for transfers between devices, body(): lax.psum_scatter(partial_value.reshape(owners, capacity, width).astype(jn...  80.3 us
    psum x1, waiting for transfers between devices, body(): lax.psum(sketch_part.astype(jnp.bfloat16), 'dp').astype(jnp.float32)  47.3 us
    gather x1, local copies, waits for them, and re-layouts, body(): features[source_token].reshape(owners, capacity, features.shape[1])  16.4 us
    another operation x3, other arithmetic, body(): jnp.linalg.cholesky(gram_matrix(sketch_full) + ridge_term * eye_matrix)  12.4 us
    all_gather x1, waiting for transfers between devices, body(): features = lax.all_gather(tokens, 'dp', axis=1, tiled=True)  12.2 us
    all_to_all x1, starting transfers between devices, body(): lax.all_to_all(count_wire, 'expert', split_axis=0, concat_axis=0, tiled=T...  12.1 us
    all_to_all x1, starting transfers between devices, body(): lax.all_to_all(sums, 'expert', split_axis=0, concat_axis=0, tiled=True)  10.8 us
  transfers between devices with their start and end apart: 6, of which 4 were waited for; matrix products, arithmetic and copies ran while one was open for 12% of the time, Pallas kernels for 0%

commit v1 on v0

--- a/solution.py
+++ b/solution.py
@@ -63,7 +63,9 @@
     sketch_part = jnp.dot(hidden_block, sketch_basis, preferred_element_type=jnp.float32)
     sketch_width = sketch_part.shape[1]
     eye_matrix = jnp.eye(sketch_width, dtype=jnp.float32)
-    sketch_full = lax.psum(sketch_part.astype(jnp.bfloat16), "dp").astype(jnp.float32)
+    sketch_full = jnp.sum(lax.all_gather(sketch_part.astype(jnp.bfloat16), "dp"), axis=0).astype(
+        jnp.float32
+    )
     lower_factor = jnp.linalg.cholesky(gram_matrix(sketch_full) + ridge_term * eye_matrix)
     projected = jnp.dot(
         sketch_full.T, hidden_block.astype(jnp.float32), precision=lax.Precision.HIGHEST

time: 464 us -> 445 us (0.959)
  waiting for transfers between devices: 323 us -> 302 us
    psum x1 -> x0, waiting for transfers between devices: 47.3 us -> none  [body(): lax.psum(sketch_part.astype(jnp.bfloat16), 'dp').astype(jnp.float32)]
    all_gather x0 -> x1, waiting for transfers between devices: none -> 26 us  [body(): lax.all_gather(sketch_part.astype(jnp.bfloat16), 'dp')]
  transfers between devices with their start and end apart: 6 -> 6, of which waited for: 4 -> 4; matrix products, arithmetic and copies ran while one was open for 12% -> 13% of each run, Pallas kernels for 0% -> 0%
where the time goes in v1:
time: 445 us; the launch traced here: 444 us
  waiting for transfers between devices  302 us (68%)
  other arithmetic  36.5 us (8%)
  starting transfers between devices  34.1 us (8%)
  local copies, waits for them, and re-layouts  31.5 us (7%)
  matrix products  26.1 us (6%)
  between operations  14 us (3%)
    all_to_all x1, waiting for transfers between devices, body(): lax.all_to_all(outgoing, 'expert', split_axis=0, concat_axis=0, tiled=True)  183 us
    reduce_scatter x1, waiting for transfers between devices, body(): lax.psum_scatter(partial_value.reshape(owners, capacity, width).astype(jn...  80.3 us
    all_gather x1, waiting for transfers between devices, body(): lax.all_gather(sketch_part.astype(jnp.bfloat16), 'dp')  26 us
    gather x1, local copies, waits for them, and re-layouts, body(): features[source_token].reshape(owners, capacity, features.shape[1])  16.4 us
    another operation x3, other arithmetic, body(): jnp.linalg.cholesky(gram_matrix(sketch_full) + ridge_term * eye_matrix)  13.2 us
    all_gather x1, waiting for transfers between devices, body(): features = lax.all_gather(tokens, 'dp', axis=1, tiled=True)  12.2 us
    all_to_all x1, starting transfers between devices, body(): lax.all_to_all(count_wire, 'expert', split_axis=0, concat_axis=0, tiled=T...  12.1 us
    all_to_all x1, starting transfers between devices, body(): lax.all_to_all(sums, 'expert', split_axis=0, concat_axis=0, tiled=True)  10.8 us
  transfers between devices with their start and end apart: 6, of which 4 were waited for; matrix products, arithmetic and copies ran while one was open for 13% of the time, Pallas kernels for 0%

profile of v1, /device:TPU:8, one launch (start us, length us, event | category | flops | bytes accessed | tf_op | source)
XLA Modules:
  0.0 444.1 jit_solution(951218488871664643)
XLA Ops:
  7.2 0.0 all-gather.4.cloned.1.call-start
  7.2 0.7 all-gather.4.cloned.1.call-update
  7.9 1.0 copy.21
  8.9 0.1 eq.33
  9.0 0.1 eq.29
  9.1 1.2 reduce-window.6
  10.3 0.2 slice_reduce_fusion
  10.6 0.2 convert_reduce_fusion
  10.8 0.7 copy.22
  11.5 12.1 %all-to-all-start = ((bf16[64,1,1]{2,1,0:T(2,128)(2,1)}), bf16[64,1,1]{2,1,0:T(2,128)(2,1)S(1)}, u32[]{:S(2)}, u32[]{:S(2)}) async-start(bf16[64,1,1]{2,1,0:T(2,128)(2,1)} %copy.22), calls=%async_computation | async-start | bytes 65536 | tf_op jit(solution)/shard_map/all_to_all | solution.py:34
  23.6 0.7 broadcast_multiply_fusion
  24.3 0.1 copy.23
  24.5 0.1 mul.28
  24.6 2.4 scatter_custom_fusion
  27.1 12.2 %all-gather.4.cloned.1.call-done = bf16[128,4096]{1,0:T(8,128)(2,1)} async-done(((bf16[128,1024]{1,0:T(8,128)(2,1)}), bf16[128,4096]{1,0:T(8,128)(2,1)}) %all-gather.4.cloned.1.call-update) | async-done | bytes 1048592 | tf_op jit(solution)/shard_map/all_gather | solution.py:30
  39.2 16.4 %gather_fusion = bf16[1024,4096]{1,0:T(8,128)(2,1)} fusion(bf16[128,4096]{1,0:T(8,128)(2,1)} %all-gather.4.cloned.1.call-done, s32[1024]{0:T(1024)S(1)} %fusion.15), kind=kCustom, calls=%fused_computation | custom fusion | bytes 16781312 | tf_op jit(solution)/shard_map/gather | solution.py:31
  55.7 10.8 %all-to-all-start.1 = ((bf16[64,16,4096]{2,1,0:T(8,128)(2,1)}), bf16[64,16,4096]{2,1,0:T(8,128)(2,1)}, u32[]{:S(2)}, u32[]{:S(2)}) async-start(bf16[64,16,4096]{2,1,0:T(8,128)(2,1)} %bitcast.61), calls=%async_computation.1 | async-start | bytes 16777216 | tf_op jit(solution)/shard_map/all_to_all | solution.py:33
  66.4 0.2 reduce-scatter.2.cloned.1.call-start
  66.7 1.2 convert_reduce_fusion.1
  67.9 0.1 iota_compare_fusion.5
  68.0 182.8 %all-to-all-done.1 = bf16[64,16,4096]{2,1,0:T(8,128)(2,1)} async-done(((bf16[64,16,4096]{2,1,0:T(8,128)(2,1)}), bf16[64,16,4096]{2,1,0:T(8,128)(2,1)}, u32[]{:S(2)}, u32[]{:S(2)}) %all-to-all-start.1) | async-done | bytes 8388640 | tf_op jit(solution)/shard_map/all_to_all | solution.py:33
  250.8 7.2 %broadcast_select_fusion = bf16[64,16,4096]{2,1,0:T(8,128)(2,1)} fusion(bf16[64,16,4096]{2,1,0:T(8,128)(2,1)} %all-to-all-done.1, pred[64,16]{1,0:T(8,128)(4,1)S(1)} %iota_compare_fusion.5), kind=kLoop, calls=%fused_computation.3 | loop fusion | flops 4194304 | bytes 16778240 | tf_op jit(solution)/shard_map/jit(_where)/select_n | solution.py:39
  258.0 8.0 %fusion.3 = f32[1024,384]{1,0:T(8,128)S(1)} fusion(bf16[1024,4096]{1,0:T(8,128)(2,1)} %bitcast.62, bf16[1,4096,384]{2,1,0:T(8,128)(2,1)} %param.10), kind=kOutput, calls=%fused_computation.8 | convolution fusion | flops 3221225472 | bytes 13107200 | tf_op jit(solution)/shard_map/dot_general | solution.py:45
  266.0 4.6 %multiply_convert_fusion = bf16[1024,384]{1,0:T(8,128)(2,1)S(1)} fusion(f32[1024,384]{1,0:T(8,128)S(1)} %fusion.3, bf16[1024,4096]{1,0:T(8,128)(2,1)S(1)} %bitcast.63, bf16[1,4096,384]{2,1,0:T(8,128)(2,1)S(1)} %copy-done.6), kind=kOutput, calls=%fused_computation.10 | convolution fusion | flops 3223584768 | bytes 13893632 | tf_op jit(solution)/shard_map/dot_general | solution.py:46
  270.6 0.9 copy-done.2
  271.5 6.6 %convolution_convert_fusion = bf16[64,16,4096]{2,1,0:T(8,128)(2,1)} fusion(bf16[64,16,384]{2,1,0:T(8,128)(2,1)S(1)} %bitcast.64, bf16[1,384,4096]{2,1,0:T(8,128)(2,1)S(1)} %copy-done), kind=kOutput, calls=%fused_computation.4 | convolution fusion | flops 3225419776 | bytes 12320768 | tf_op jit(solution)/shard_map/dot_general | solution.py:48
  278.1 0.0 reduce-scatter.2.cloned.1.call-update
  278.2 80.3 %reduce-scatter.2.cloned.1.call-done = bf16[64,16,1024]{2,1,0:T(8,128)(2,1)} async-done(((bf16[64,16,4096]{2,1,0:T(8,128)(2,1)}), bf16[64,16,1024]{2,1,0:T(8,128)(2,1)}) %reduce-scatter.2.cloned.1.call-update) | async-done | bytes 2097168 | tf_op jit(solution)/shard_map/reduce_scatter | solution.py:49
  358.5 10.8 %all-to-all-start.2 = ((bf16[64,16,1024]{2,1,0:T(8,128)(2,1)}), bf16[64,16,1024]{2,1,0:T(8,128)(2,1)}, u32[]{:S(2)}, u32[]{:S(2)}) async-start(bf16[64,16,1024]{2,1,0:T(8,128)(2,1)} %reduce-scatter.2.cloned.1.call-done), calls=%async_computation.3 | async-start | bytes 4194304 | tf_op jit(solution)/shard_map/all_to_all | solution.py:55
  369.2 0.3 all-gather.6.cloned.1.call-start
  369.5 2.2 convolution_convert_fusion.1
  371.7 0.0 all-gather.6.cloned.1.call-update
  371.7 0.8 copy.27
  372.5 26.0 %all-gather.6.cloned.1.call-done = bf16[4096,128]{1,0:T(8,128)(2,1)} async-done(((bf16[1024,128]{1,0:T(8,128)(2,1)}), bf16[4096,128]{1,0:T(8,128)(2,1)}) %all-gather.6.cloned.1.call-update) | async-done | bytes 1048592 | tf_op jit(solution)/shard_map/all_gather | solution.py:66
  398.5 1.5 reduce_sum.35
  400.0 0.3 fusion.20
  400.2 0.1 copy.26
  400.3 0.7 fusion.13
  401.0 12.5 %cholesky.17 = f32[128,128]{1,0:T(8,128)S(1)} custom-call(f32[128,128]{1,0:T(8,128)} %fusion.13), custom_call_target="Cholesky" | custom-call | tf_op jit(solution)/shard_map/jit(cholesky)/cholesky | solution.py:69
  413.6 0.6 compare_reduce_fusion
  414.2 0.7 fusion.10
  414.9 9.8 %custom-call.7 = f32[1,128,128]{1,2,0:T(8,128)S(1)} custom-call(f32[1,128,128]{2,1,0:T(8,128)S(1)} %fusion.10), custom_call_target="InvertDiagBlocksLowerTriangular" | custom-call | tf_op jit(solution)/shard_map/jit(_solve_triangular)/triangular_solve | solution.py:73
  424.7 1.5 fusion.21
  426.2 1.0 convolution_bitcast_fusion
  427.2 5.4 %gather_fusion.1 = bf16[512,1024]{1,0:T(8,128)(2,1)} fusion(bf16[1024,1024]{1,0:T(8,128)(2,1)} %bitcast.11, s32[1024]{0:T(1024)S(1)} %pad_clamp_fusion), kind=kCustom, calls=%fused_computation.1 | custom fusion | bytes 2099200 | tf_op jit(solution)/shard_map/gather | solution.py:56
  432.6 2.3 reshape.115
  434.8 1.9 fusion.19
  436.8 0.8 copy.32
  (24 shorter events, 0.2 us)
Async XLA Ops:
  7.2 264.3 %copy-start = (bf16[1,384,4096]{2,1,0:T(8,128)(2,1)S(1)}, bf16[1,384,4096]{2,1,0:T(8,128)(2,1)}, u32[]{:S(2)}) copy-start(bf16[1,384,4096]{2,1,0:T(8,128)(2,1)} %param.12) | copy-start | bytes 9437188
  7.2 32.0 %all-gather.4.cloned.1.call-start = ((), (), s32[]{:S(2)}) async-start(), calls=%async_computation.4 | async-start | bytes 1310720 | tf_op jit(solution)/shard_map/all_gather | solution.py:30
  11.5 44.1 %all-to-all-start = ((bf16[64,1,1]{2,1,0:T(2,128)(2,1)}), bf16[64,1,1]{2,1,0:T(2,128)(2,1)S(1)}, u32[]{:S(2)}, u32[]{:S(2)}) async-start(bf16[64,1,1]{2,1,0:T(2,128)(2,1)} %copy.22), calls=%async_computation | async-start | bytes 65536 | tf_op jit(solution)/shard_map/all_to_all | solution.py:34
  55.7 195.1 %all-to-all-start.1 = ((bf16[64,16,4096]{2,1,0:T(8,128)(2,1)}), bf16[64,16,4096]{2,1,0:T(8,128)(2,1)}, u32[]{:S(2)}, u32[]{:S(2)}) async-start(bf16[64,16,4096]{2,1,0:T(8,128)(2,1)} %bitcast.61), calls=%async_computation.1 | async-start | bytes 16777216 | tf_op jit(solution)/shard_map/all_to_all | solution.py:33
  66.4 292.0 %reduce-scatter.2.cloned.1.call-start = ((), (), s32[]{:S(2)}) async-start(), calls=%async_computation.5 | async-start | bytes 10485760 | tf_op jit(solution)/shard_map/reduce_scatter | solution.py:49
  258.0 8.0 %copy-start.1 = (bf16[64,16,4096]{2,1,0:T(8,128)(2,1)S(1)}, bf16[64,16,4096]{2,1,0:T(8,128)(2,1)}, u32[]{:S(2)}) copy-start(bf16[64,16,4096]{2,1,0:T(8,128)(2,1)} %broadcast_select_fusion) | copy-start | bytes 25165828
  258.0 8.0 %copy-start.6 = (bf16[1,4096,384]{2,1,0:T(8,128)(2,1)S(1)}, bf16[1,4096,384]{2,1,0:T(8,128)(2,1)}, u32[]{:S(2)}) copy-start(bf16[1,4096,384]{2,1,0:T(8,128)(2,1)} %param.11) | copy-start | bytes 9437188
  270.6 0.9 copy-start.2
  278.1 91.4 %copy-start.3 = (bf16[384,128]{1,0:T(8,128)(2,1)S(1)}, bf16[384,128]{1,0:T(8,128)(2,1)}, u32[]{:S(2)}) copy-start(bf16[384,128]{1,0:T(8,128)(2,1)} %param.13) | copy-start | bytes 294916
  278.2 93.6 %copy-start.5 = (f32[128,4]{0,1:T(4,128)S(1)}, f32[128,4]{0,1:T(4,128)}, u32[]{:S(2)}) copy-start(f32[128,4]{0,1:T(4,128)} %param.9) | copy-start | bytes 6148
  358.5 68.8 %all-to-all-start.2 = ((bf16[64,16,1024]{2,1,0:T(8,128)(2,1)}), bf16[64,16,1024]{2,1,0:T(8,128)(2,1)}, u32[]{:S(2)}, u32[]{:S(2)}) async-start(bf16[64,16,1024]{2,1,0:T(8,128)(2,1)} %reduce-scatter.2.cloned.1.call-done), calls=%async_computation.3 | async-start | bytes 4194304 | tf_op jit(solution)/shard_map/all_to_all | solution.py:55
  369.2 29.3 %all-gather.6.cloned.1.call-start = ((), (), s32[]{:S(2)}) async-start(), calls=%async_computation.6 | async-start | bytes 1310720 | tf_op jit(solution)/shard_map/all_gather | solution.py:66
  427.2 7.6 %copy-start.4 = (bf16[128,4,1]{1,2,0:T(2,128)(2,1)S(1)}, bf16[128,4,1]{1,2,0:T(2,128)(2,1)}, u32[]{:S(2)}) copy-start(bf16[128,4,1]{1,2,0:T(2,128)(2,1)} %copy.27) | copy-start | bytes 3076
Sparse Core Ops, SparseCore 0:
  9.8 29.3 all-gather.3
  278.3 80.1 reduce-scatter.1
  372.4 25.9 all-gather.5
